TPU v7x, 32 devices: a whole 2x2x4 slice. The times are simulated.
32 devices in a mesh: grp: 4 (over z), dev: 8 (over y, x, core).
Axes of the slice: x: 2, y: 2, z: 4, core: 2. Of those that a mesh axis runs over, the one named last changes fastest.
Arguments:
- sources: bfloat16 [8, 131072], P(None, ('grp', 'dev')), may hold values from -6 to 6
- boundary_impedance_input: float32 [8, 256], replicated, may hold values from -6 to 6
- leaf_inverse: bfloat16 [131072, 2048], P(('grp', 'dev')), may hold values from -0.1875 to 0.1875
- leaf_flux: bfloat16 [131072, 256], P(('grp', 'dev')), may hold values from -0.1875 to 0.1875
- leaf_lift: bfloat16 [16384, 2048], P(('grp', 'dev')), may hold values from -0.375 to 0.375
- node_schur: float32 [128, 64, 128], P(('grp', 'dev')), may hold values from -0.375 to 0.375
- node_spread: float32 [128, 64, 256], P(('grp', 'dev')), may hold values from -0.1875 to 0.1875
- node_lift: float32 [128, 128, 128], P(('grp', 'dev')), may hold values from -0.25 to 0.25
Outputs:
- field: float32 [8, 262144], P(None, ('grp', 'dev'))
All inputs are finite; a program needn't handle non-finite values.
Results may differ from a plain program's by a relative error of at most 0.0025.
Values sent between devices are 32-bit elements; how exact they have to be, the bound alone decides.
A program may use at most 128 MiB of HBM per device.

v0:
```python
import jax
import jax.numpy as jnp
from jax import lax
from jax.sharding import PartitionSpec as P


def complex_mul(vector, matrix):
    inner = matrix.shape[1]
    cols = matrix.shape[2] // 2
    hp = lax.Precision.HIGHEST
    from_real = jnp.einsum("nsa,nab->nsb", vector[..., :inner], matrix, precision=hp)
    from_imag = jnp.einsum("nsa,nab->nsb", vector[..., inner:], matrix, precision=hp)
    return jnp.concatenate(
        [
            from_real[..., :cols] - from_imag[..., cols:],
            from_real[..., cols:] + from_imag[..., :cols],
        ],
        -1,
    )


def select_component(vector, start, stop):
    half = vector.shape[-1] // 2
    return jnp.concatenate([vector[..., start:stop], vector[..., half + start : half + stop]], -1)


def join_parts(first, second):
    half_one = first.shape[-1] // 2
    half_two = second.shape[-1] // 2
    return jnp.concatenate(
        [
            first[..., :half_one],
            second[..., :half_two],
            first[..., half_one:],
            second[..., half_two:],
        ],
        -1,
    )


def merge_pair(left_out, right_out, schur, spread):
    width = left_out.shape[-1] // 4
    jump = complex_mul(
        select_component(right_out, width, 2 * width)
        - select_component(left_out, width, 2 * width),
        schur,
    )
    parent = join_parts(
        select_component(left_out, 0, width), select_component(right_out, 0, width)
    ) + complex_mul(jump, spread)
    return (jump, parent)


def split_children(incoming, iface):
    width = incoming.shape[-1] // 4
    return (
        join_parts(select_component(incoming, 0, width), iface),
        join_parts(select_component(incoming, width, 2 * width), iface),
    )


def ascend(outgoing, schur, spread):
    levels = outgoing.shape[0].bit_length() - 1
    jumps = []
    for tier_index in range(levels):
        half_step = 2**tier_index
        jump, outgoing = merge_pair(
            outgoing[0::2],
            outgoing[1::2],
            schur[half_step :: 2 * half_step],
            spread[half_step :: 2 * half_step],
        )
        jumps.append(jump)
    return (outgoing, jumps)


def descend(incoming, jumps, lift):
    for tier_index in reversed(range(len(jumps))):
        half_step = 2**tier_index
        iface = complex_mul(incoming, lift[half_step :: 2 * half_step]) + jumps[tier_index]
        left_in, right_in = split_children(incoming, iface)
        incoming = jnp.stack([left_in, right_in], 1).reshape(
            -1, incoming.shape[1], incoming.shape[2]
        )
    return incoming


def body(
    sources,
    boundary_impedance_input,
    leaf_inverse,
    leaf_flux,
    leaf_lift,
    node_schur,
    node_spread,
    node_lift,
):
    source_count = sources.shape[0]
    leaves_here = node_schur.shape[0]
    cell_count = leaf_inverse.shape[1] // 2
    interface_edge_count = leaf_flux.shape[1] // 2
    source_blocks = sources.reshape(source_count, leaves_here, cell_count)
    leaf_out = jnp.einsum(
        "slc,lce->lse",
        source_blocks,
        leaf_flux.reshape(leaves_here, cell_count, 2 * interface_edge_count),
        preferred_element_type=jnp.float32,
    )
    local_root, local_jumps = ascend(leaf_out, node_schur, node_spread)
    place = lax.axis_index("grp") * lax.axis_size("dev") + lax.axis_index("dev")
    roots = lax.all_gather(local_root, ("grp", "dev"), axis=0, tiled=True)
    schur_all, spread_all, lift_all = (
        lax.all_gather(node_schur[0:1], ("grp", "dev"), axis=0, tiled=True),
        lax.all_gather(node_spread[0:1], ("grp", "dev"), axis=0, tiled=True),
        lax.all_gather(node_lift[0:1], ("grp", "dev"), axis=0, tiled=True),
    )
    top_out, tree_jumps = ascend(roots, schur_all, spread_all)
    incoming_all = descend(boundary_impedance_input[None], tree_jumps, lift_all)
    device_in = lax.dynamic_slice_in_dim(incoming_all, place, 1, 0)
    incoming = descend(device_in, local_jumps, node_lift)
    leaf_input_values = incoming.astype(jnp.bfloat16)
    particular = jnp.einsum(
        "vfz,fzo->vfo",
        source_blocks,
        leaf_inverse.reshape(leaves_here, cell_count, 2 * cell_count),
        preferred_element_type=jnp.float32,
    )
    lifting_operator = leaf_lift.reshape(leaves_here, interface_edge_count, 2 * cell_count)
    from_real = jnp.einsum(
        "kpi,kih->pkh",
        leaf_input_values[..., :interface_edge_count],
        lifting_operator,
        preferred_element_type=jnp.float32,
    )
    from_imag = jnp.einsum(
        "kpi,kih->pkh",
        leaf_input_values[..., interface_edge_count:],
        lifting_operator,
        preferred_element_type=jnp.float32,
    )
    lifted = jnp.concatenate(
        [
            from_real[..., :cell_count] - from_imag[..., cell_count:],
            from_real[..., cell_count:] + from_imag[..., :cell_count],
        ],
        -1,
    )
    field = particular + lifted
    return field.reshape(source_count, leaves_here * 2 * cell_count)


def solution(mesh):
    in_specs = (
        P(None, ("grp", "dev")),
        P(),
        P(("grp", "dev"), None),
        P(("grp", "dev"), None),
        P(("grp", "dev"), None),
        P(("grp", "dev"), None, None),
        P(("grp", "dev"), None, None),
        P(("grp", "dev"), None, None),
    )
    out_specs = P(None, ("grp", "dev"))
    return jax.shard_map(body, mesh=mesh, in_specs=in_specs, out_specs=out_specs, check_vma=False)
```

profile of v0, /device:TPU:0, one launch (start us, length us, event | category | flops | bytes accessed | tf_op | source)
XLA Modules:
  0.0 212.5 jit_solution(15684005119780731152)
XLA Ops:
  6.5 1.5 slice.828
  8.1 1.5 slice.833
  9.7 1.5 slice.768
  11.2 2.0 fusion.166
  13.3 0.2 fusion.77
  13.6 0.2 fusion.79
  13.8 0.2 fusion.53
  14.0 0.2 fusion.55
  14.6 0.2 convolution_bitcast_fusion.9
  15.3 44.0 %all_gather.13 = f32[32,8,256]{2,1,0:T(8,128)S(1)} all-gather(f32[1,8,256]{2,1,0:T(8,128)S(1)} %maximum_add_fusion.8), channel_id=1, replica_groups=mesh['grp'=4,'dev'=8] {'grp','dev'}, dimensions={0}, use_global_device_ids=true | all-gather | bytes 270336 | tf_op jit(solution)/shard_map/all_gather | solution.py:111
  59.7 7.2 %all-gather.6.cloned.1.call-done = f32[32,64,128]{2,1,0:T(8,128)} async-done(((f32[1,64,128]{2,1,0:T(8,128)}), f32[32,64,128]{2,1,0:T(8,128)}) %all-gather.6.cloned.1.call-update) | async-done | bytes 1048592 | tf_op jit(solution)/shard_map/all_gather | solution.py:113
  66.9 1.6 fusion.19
  68.5 1.6 fusion.17
  70.2 54.9 %all-gather.8.cloned.1.call-done = f32[32,64,256]{2,1,0:T(8,128)} async-done(((f32[1,64,256]{2,1,0:T(8,128)}), f32[32,64,256]{2,1,0:T(8,128)}) %all-gather.8.cloned.1.call-update) | async-done | bytes 2097168 | tf_op jit(solution)/shard_map/all_gather | solution.py:114
  125.1 1.9 fusion.5
  127.0 2.0 fusion.7
  129.5 0.3 fusion.31
  129.8 0.4 fusion.29
  130.3 0.4 fusion.15
  130.7 0.4 fusion.13
  131.4 0.2 fusion.51
  131.6 0.3 fusion.49
  132.0 0.2 fusion.27
  132.2 0.2 fusion.25
  132.8 0.2 fusion.73
  133.0 0.2 fusion.71
  133.3 0.2 fusion.47
  133.5 0.2 fusion.45
  134.0 0.2 convolution_bitcast_fusion.7
  134.3 48.9 %all-gather.4.cloned.1.call-done = f32[32,128,128]{2,1,0:T(8,128)} async-done(((f32[1,128,128]{2,1,0:T(8,128)}), f32[32,128,128]{2,1,0:T(8,128)}) %all-gather.4.cloned.1.call-update) | async-done | bytes 2097168 | tf_op jit(solution)/shard_map/all_gather | solution.py:115
  183.3 1.1 convolution_bitcast_fusion.11
  184.4 1.0 convolution_bitcast_fusion.12
  185.8 1.1 fusion.43
  186.9 1.1 fusion.41
  188.5 1.3 fusion.23
  189.8 1.3 fusion.21
  191.5 0.5 fusion.11
  192.0 0.5 fusion.9
  193.0 1.0 fusion.3
  194.0 1.0 fusion.1
  195.5 0.2 convolution_bitcast_fusion.6
  195.7 0.2 convolution_bitcast_fusion.5
  196.2 0.2 fusion.37
  196.5 0.2 fusion.39
  197.1 0.4 convolution_bitcast_fusion
  197.5 0.4 convolution_bitcast_fusion.1
  197.9 0.4 copy-done.7
  198.3 7.7 %fusion = f32[8,4,2048]{2,0,1:T(8,128)} fusion(bf16[4,1024,2048]{2,1,0:T(8,128)(2,1)} %bitcast.144, bf16[8,4,1024]{2,0,1:T(8,128)(2,1)S(1)} %bitcast.159, f32[8,4,1024]{2,0,1:T(8,128)S(1)} %get-tuple-element.6, f32[8,4,1024]{2,0,1:T(8,128)S(1)} %get-tuple-element.5), kind=kOutput, calls=%fused_computation.3 | convolution fusion | flops 134348800 | bytes 17367040 | tf_op jit(solution)/shard_map/vfz,fzo->vfo/dot_general | solution.py:122
  (118 shorter events, 6.5 us)
Async XLA Ops:
  6.5 190.6 %copy-start = (bf16[512,2048]{1,0:T(8,128)(2,1)S(1)}, bf16[512,2048]{1,0:T(8,128)(2,1)}, u32[]{:S(2)}) copy-start(bf16[512,2048]{1,0:T(8,128)(2,1)} %param.12) | copy-start | bytes 6291460
  6.5 6.8 %copy-start.6 = (f32[4,64,128]{2,1,0:T(8,128)S(1)}, f32[4,64,128]{2,1,0:T(8,128)}, u32[]{:S(2)}) copy-start(f32[4,64,128]{2,1,0:T(8,128)} %param.13) | copy-start | bytes 393220
  6.5 7.3 %copy-start.5 = (f32[4,64,256]{2,1,0:T(8,128)S(1)}, f32[4,64,256]{2,1,0:T(8,128)}, u32[]{:S(2)}) copy-start(f32[4,64,256]{2,1,0:T(8,128)} %param.14) | copy-start | bytes 786436
  6.5 60.3 %all-gather.6.cloned.1.call-start = ((), (), s32[]{:S(2)}) async-start(), calls=%async_computation.1 | async-start | bytes 1081344 | tf_op jit(solution)/shard_map/all_gather | solution.py:113
  8.1 117.0 %all-gather.8.cloned.1.call-start = ((), (), s32[]{:S(2)}) async-start(), calls=%async_computation.2 | async-start | bytes 2162688 | tf_op jit(solution)/shard_map/all_gather | solution.py:114
  9.6 173.6 %all-gather.4.cloned.1.call-start = ((), (), s32[]{:S(2)}) async-start(), calls=%async_computation | async-start | bytes 2162688 | tf_op jit(solution)/shard_map/all_gather | solution.py:115
  13.2 46.3 %copy-start.8 = (f32[8,256]{1,0:T(8,128)S(1)}, f32[8,256]{1,0:T(8,128)}, u32[]{:S(2)}) copy-start(f32[8,256]{1,0:T(8,128)} %param.9) | copy-start | bytes 24580
  125.1 4.4 %copy-start.3 = (f32[32,64,128]{2,1,0:T(8,128)S(1)}, f32[32,64,128]{2,1,0:T(8,128)}, u32[]{:S(2)}) copy-start(f32[32,64,128]{2,1,0:T(8,128)} %all-gather.6.cloned.1.call-done) | copy-start | bytes 3145732
  127.0 3.2 %copy-start.2 = (f32[32,64,256]{2,1,0:T(8,128)S(1)}, f32[32,64,256]{2,1,0:T(8,128)}, u32[]{:S(2)}) copy-start(f32[32,64,256]{2,1,0:T(8,128)} %all-gather.8.cloned.1.call-done) | copy-start | bytes 6291460
  183.3 8.2 %copy-start.1 = (f32[32,128,128]{2,1,0:T(8,128)S(1)}, f32[32,128,128]{2,1,0:T(8,128)}, u32[]{:S(2)}) copy-start(f32[32,128,128]{2,1,0:T(8,128)} %all-gather.4.cloned.1.call-done) | copy-start | bytes 6291460
  194.0 1.5 copy-start.4
  197.5 0.8 copy-start.7
Sparse Core Ops, SparseCore 0:
  10.2 56.6 all-gather.5
  69.7 55.3 all-gather.7
  128.0 55.2 all-gather.3
where the time goes:
time: 213 us
  waiting for transfers between devices  111 us (52%)
  blocking collectives  44 us (21%)
  matrix products  33.3 us (16%)
  between operations  13.4 us (6%)
  local copies, waits for them, and re-layouts  6.94 us (3%)
  other arithmetic  3.7 us (2%)
    all_gather x1, waiting for transfers between devices, body(): lax.all_gather(node_spread[0:1], ('grp', 'dev'), axis=0, tiled=True)  54.9 us
    all_gather x1, waiting for transfers between devices, body(): lax.all_gather(node_lift[0:1], ('grp', 'dev'), axis=0, tiled=True)  48.9 us
    all_gather x1, blocking collectives, body(): roots = lax.all_gather(local_root, ('grp', 'dev'), axis=0, tiled=True)  44 us
    dot_general x20, matrix products, complex_mul(): jnp.einsum('nsa,nab->nsb', vector[..., inner:], matrix, precision=hp)  11.7 us
    dot_general x20, matrix products, complex_mul(): jnp.einsum('nsa,nab->nsb', vector[..., :inner], matrix, precision=hp)  11.1 us
    dot_general x1, matrix products, body(): jnp.einsum('vfz,fzo->vfo', source_blocks, leaf_inverse.reshape(leaves_her...  7.68 us
    all_gather x1, waiting for transfers between devices, body(): lax.all_gather(node_schur[0:1], ('grp', 'dev'), axis=0, tiled=True)  7.18 us
  transfers between devices with their start and end apart: 3, of which 3 were waited for; matrix products, arithmetic and copies ran while one was open for 9% of the time, Pallas kernels for 0%

commit v1 on v0

--- a/solution.py
+++ b/solution.py
@@ -1,7 +1,25 @@
+import functools
 import jax
 import jax.numpy as jnp
 from jax import lax
 from jax.sharding import PartitionSpec as P
+
+
+def _carry_modes(local_x, ndim_at):
+    r1, inter = (lax.axis_size(("grp", "dev")), lax.axis_index(("grp", "dev")))
+    m_next, prior = (local_x, 1)
+    while prior < r1:
+        x_new = lax.ppermute(
+            m_next, ("grp", "dev"), tuple(((tick, tick ^ prior) for tick in range(r1)))
+        )
+        local_next = jnp.concatenate([m_next, x_new], axis=ndim_at)
+        found_now = jnp.concatenate([x_new, m_next], axis=ndim_at)
+        m_next = jnp.where(inter & prior == 0, local_next, found_now)
+        prior = 2 * prior
+    return m_next
+
+
+convert_point = functools.partial(_carry_modes, ndim_at=0)
 
 
 def complex_mul(vector, matrix):
@@ -110,7 +128,7 @@
     place = lax.axis_index("grp") * lax.axis_size("dev") + lax.axis_index("dev")
     roots = lax.all_gather(local_root, ("grp", "dev"), axis=0, tiled=True)
     schur_all, spread_all, lift_all = (
-        lax.all_gather(node_schur[0:1], ("grp", "dev"), axis=0, tiled=True),
+        convert_point(node_schur[0:1]),
         lax.all_gather(node_spread[0:1], ("grp", "dev"), axis=0, tiled=True),
         lax.all_gather(node_lift[0:1], ("grp", "dev"), axis=0, tiled=True),
     )

time: 213 us -> 164 us (0.77)
  waiting for transfers between devices: 111 us -> 60.7 us
  starting transfers between devices: 0.09 us -> 5.03 us
  blocking collectives: 44 us -> 41.7 us
  matrix products: 33.3 us -> 31.1 us
    all_gather x1, waiting for transfers between devices: 54.9 us -> 0.02 us  [body(): lax.all_gather(node_spread[0:1], ('grp', 'dev'), axis=0, tiled=True)]
    ppermute x0 -> x5, waiting for transfers between devices: none -> 37.5 us  [_carry_modes(): lax.ppermute(m_next, ('grp', 'dev'), tuple(((tick, tick ^ prior) for tick...]
    all_gather x1, waiting for transfers between devices: 48.9 us -> 23.1 us  [body(): lax.all_gather(node_lift[0:1], ('grp', 'dev'), axis=0, tiled=True)]
    all_gather x1 -> x0, waiting for transfers between devices: 7.18 us -> none  [body(): lax.all_gather(node_schur[0:1], ('grp', 'dev'), axis=0, tiled=True)]
    ppermute x0 -> x5, starting transfers between devices: none -> 4.98 us  [_carry_modes(): lax.ppermute(m_next, ('grp', 'dev'), tuple(((tick, tick ^ prior) for tick...]
    all_gather x1, blocking collectives: 44 us -> 41.7 us  [body(): roots = lax.all_gather(local_root, ('grp', 'dev'), axis=0, tiled=True)]
  transfers between devices with their start and end apart: 3 -> 7, of which waited for: 3 -> 4; matrix products, arithmetic and copies ran while one was open for 9% -> 11% of each run, Pallas kernels for 0% -> 0%
where the time goes in v1:
time: 164 us
  waiting for transfers between devices  60.7 us (37%)
  blocking collectives  41.7 us (25%)
  matrix products  31.1 us (19%)
  between operations  13.9 us (8%)
  local copies, waits for them, and re-layouts  7.23 us (4%)
  starting transfers between devices  5.03 us (3%)
  other arithmetic  3.9 us (2%)
    all_gather x1, blocking collectives, body(): roots = lax.all_gather(local_root, ('grp', 'dev'), axis=0, tiled=True)  41.7 us
    ppermute x5, waiting for transfers between devices, _carry_modes(): lax.ppermute(m_next, ('grp', 'dev'), tuple(((tick, tick ^ prior) for tick...  37.5 us
    all_gather x1, waiting for transfers between devices, body(): lax.all_gather(node_lift[0:1], ('grp', 'dev'), axis=0, tiled=True)  23.1 us
    dot_general x20, matrix products, complex_mul(): jnp.einsum('nsa,nab->nsb', vector[..., inner:], matrix, precision=hp)  10.6 us
    dot_general x20, matrix products, complex_mul(): jnp.einsum('nsa,nab->nsb', vector[..., :inner], matrix, precision=hp)  10.1 us
    dot_general x1, matrix products, body(): jnp.einsum('vfz,fzo->vfo', source_blocks, leaf_inverse.reshape(leaves_her...  7.68 us
    ppermute x5, starting transfers between devices, _carry_modes(): lax.ppermute(m_next, ('grp', 'dev'), tuple(((tick, tick ^ prior) for tick...  4.98 us
  transfers between devices with their start and end apart: 7, of which 4 were waited for; matrix products, arithmetic and copies ran while one was open for 11% of the time, Pallas kernels for 0%

profile of v1, /device:TPU:0, one launch (start us, length us, event | category | flops | bytes accessed | tf_op | source)
XLA Modules:
  0.0 163.5 jit_solution(10985557754695274797)
XLA Ops:
  6.5 1.6 %slice.833 = f32[1,64,256]{2,1,0:T(8,128)} slice(f32[4,64,256]{2,1,0:T(8,128)} %param.14), slice={[0:1], [0:64], [0:256]} | slice | bytes 131072 | tf_op jit(solution)/shard_map/slice | solution.py:132
  8.3 0.8 slice.828
  9.0 0.5 collective-permute-start
  9.5 1.5 slice.768
  11.0 2.0 %fusion.166 = f32[4,8,256]{2,1,0:T(8,128)S(1)} fusion(bf16[8,4,1024]{2,0,1:T(8,128)(2,1)} %bitcast.158, bf16[4,1024,256]{2,1,0:T(8,128)(2,1)} %bitcast.148), kind=kOutput, calls=%fused_computation.293 | convolution fusion | flops 16777216 | bytes 2195456 | tf_op jit(solution)/shard_map/slc,lce->lse/dot_general | solution.py:121
  13.2 0.2 fusion.77
  13.6 0.2 fusion.53
  14.0 0.2 copy-done.8
  14.6 0.2 convolution_bitcast_fusion.9
  15.2 2.6 %collective-permute-start.1 = (f32[2,64,128]{2,1,0:T(8,128)S(1)}, f32[2,64,128]{2,1,0:T(8,128)S(1)}, u32[]{:S(2)}, u32[]{:S(2)}) collective-permute-start(f32[2,64,128]{2,1,0:T(8,128)S(1)} %maximum_select_fusion.4), channel_id=1, source_target_pairs={{0,2},{1,3},{2,0},{3,1},{4,6},{5,7},{6,4},{7,5},{8,10},{9,11},{10,... | collective-permute-start | bytes 196616 | tf_op jit(solution)/shard_map/ppermute | solution.py:12
  17.8 2.8 %collective-permute-done.1 = f32[2,64,128]{2,1,0:T(8,128)S(1)} collective-permute-done((f32[2,64,128]{2,1,0:T(8,128)S(1)}, f32[2,64,128]{2,1,0:T(8,128)S(1)}, u32[]{:S(2)}, u32[]{:S(2)}) %collective-permute-start.1) | collective-permute-done | bytes 65568 | tf_op jit(solution)/shard_map/ppermute | solution.py:12
  20.6 1.8 %collective-permute-start.2 = (f32[4,64,128]{2,1,0:T(8,128)S(1)}, f32[4,64,128]{2,1,0:T(8,128)S(1)}, u32[]{:S(2)}, u32[]{:S(2)}) collective-permute-start(f32[4,64,128]{2,1,0:T(8,128)S(1)} %maximum_select_fusion.3), channel_id=1, source_target_pairs={{0,4},{1,5},{2,6},{3,7},{4,0},{5,1},{6,2},{7,3},{8,12},{9,13},{10,... | collective-permute-start | bytes 393224 | tf_op jit(solution)/shard_map/ppermute | solution.py:12
  22.5 41.7 %all_gather.10 = f32[32,8,256]{2,1,0:T(8,128)S(1)} all-gather(f32[1,8,256]{2,1,0:T(8,128)S(1)} %maximum_add_fusion.8), channel_id=1, replica_groups=mesh['grp'=4,'dev'=8] {'grp','dev'}, dimensions={0}, use_global_device_ids=true | all-gather | bytes 270336 | tf_op jit(solution)/shard_map/all_gather | solution.py:129
  64.4 8.7 %collective-permute-done.3 = f32[8,64,128]{2,1,0:T(8,128)S(1)} collective-permute-done((f32[8,64,128]{2,1,0:T(8,128)S(1)}, f32[8,64,128]{2,1,0:T(8,128)S(1)}, u32[]{:S(2)}, u32[]{:S(2)}) %collective-permute-start.3) | collective-permute-done | bytes 262176 | tf_op jit(solution)/shard_map/ppermute | solution.py:12
  73.5 0.7 fusion.162
  74.2 26.0 %collective-permute-done.4 = f32[16,64,128]{2,1,0:T(8,128)S(1)} collective-permute-done((f32[16,64,128]{2,1,0:T(8,128)S(1)}, f32[16,64,128]{2,1,0:T(8,128)S(1)}, u32[]{:S(2)}, u32[]{:S(2)}) %collective-permute-start.4) | collective-permute-done | bytes 524320 | tf_op jit(solution)/shard_map/ppermute | solution.py:12
  100.3 0.5 fusion.19
  100.8 0.6 fusion.17
  101.6 1.9 %fusion.5 = f32[16,8,256]{2,1,0:T(8,128)S(1)} fusion(f32[16,8,64]{2,1,0:T(8,128)S(1)} %get-tuple-element.28, f32[32,64,256]{2,1,0:T(8,128)} %all-gather.5.cloned.1.call-done), kind=kOutput, calls=%fused_computation.19 | convolution fusion | flops 25165824 | bytes 1212416 | tf_op jit(solution)/shard_map/nsa,nab->nsb/dot_general | solution.py:30
  103.5 2.0 %fusion.7 = f32[16,8,256]{2,1,0:T(8,128)S(1)} fusion(f32[16,8,64]{2,1,0:T(8,128)S(1)} %get-tuple-element.27, f32[32,64,256]{2,1,0:T(8,128)} %all-gather.5.cloned.1.call-done), kind=kOutput, calls=%fused_computation.21 | convolution fusion | flops 25165824 | bytes 1212416 | tf_op jit(solution)/shard_map/nsa,nab->nsb/dot_general | solution.py:29
  105.9 0.3 fusion.31
  106.2 0.4 fusion.29
  106.7 0.4 fusion.15
  107.1 0.4 fusion.13
  107.8 0.2 fusion.51
  108.0 0.3 fusion.49
  108.4 0.3 fusion.27
  108.7 0.2 fusion.25
  109.4 0.2 fusion.71
  109.7 0.2 fusion.47
  110.5 0.2 convolution_bitcast_fusion.7
  110.8 23.1 %all-gather.3.cloned.1.call-done = f32[32,128,128]{2,1,0:T(8,128)} async-done(((f32[1,128,128]{2,1,0:T(8,128)}), f32[32,128,128]{2,1,0:T(8,128)}) %all-gather.3.cloned.1.call-update) | async-done | bytes 2097168 | tf_op jit(solution)/shard_map/all_gather | solution.py:133
  133.9 1.1 convolution_bitcast_fusion.11
  135.1 1.0 convolution_bitcast_fusion.12
  136.5 1.1 fusion.43
  137.6 1.1 fusion.41
  139.1 1.3 fusion.23
  140.4 1.3 fusion.21
  142.1 0.5 fusion.11
  142.7 0.5 fusion.9
  143.7 1.0 fusion.3
  144.7 1.0 fusion.1
  146.9 0.2 fusion.37
  147.1 0.2 fusion.39
  147.8 0.4 convolution_bitcast_fusion
  148.2 0.4 convolution_bitcast_fusion.1
  148.6 0.4 copy-done.6
  149.0 7.7 %fusion = f32[8,4,2048]{2,0,1:T(8,128)} fusion(bf16[4,1024,2048]{2,1,0:T(8,128)(2,1)} %bitcast.144, bf16[8,4,1024]{2,0,1:T(8,128)(2,1)S(1)} %bitcast.159, f32[8,4,1024]{2,0,1:T(8,128)S(1)} %get-tuple-element.6, f32[8,4,1024]{2,0,1:T(8,128)S(1)} %get-tuple-element.5), kind=kOutput, calls=%fused_computation.3 | convolution fusion | flops 134348800 | bytes 17367040 | tf_op jit(solution)/shard_map/vfz,fzo->vfo/dot_general | solution.py:140
  (148 shorter events, 7.8 us)
Async XLA Ops:
  6.5 141.2 %copy-start = (bf16[512,2048]{1,0:T(8,128)(2,1)S(1)}, bf16[512,2048]{1,0:T(8,128)(2,1)}, u32[]{:S(2)}) copy-start(bf16[512,2048]{1,0:T(8,128)(2,1)} %param.12) | copy-start | bytes 6291460
  6.5 7.1 %copy-start.4 = (f32[4,64,256]{2,1,0:T(8,128)S(1)}, f32[4,64,256]{2,1,0:T(8,128)}, u32[]{:S(2)}) copy-start(f32[4,64,256]{2,1,0:T(8,128)} %param.14) | copy-start | bytes 786436
  6.5 6.6 %copy-start.5 = (f32[4,64,128]{2,1,0:T(8,128)S(1)}, f32[4,64,128]{2,1,0:T(8,128)}, u32[]{:S(2)}) copy-start(f32[4,64,128]{2,1,0:T(8,128)} %param.13) | copy-start | bytes 393220
  6.5 95.0 %all-gather.5.cloned.1.call-start = ((), (), s32[]{:S(2)}) async-start(), calls=%async_computation.1 | async-start | bytes 2162688 | tf_op jit(solution)/shard_map/all_gather | solution.py:132
  8.2 125.7 %all-gather.3.cloned.1.call-start = ((), (), s32[]{:S(2)}) async-start(), calls=%async_computation | async-start | bytes 2162688 | tf_op jit(solution)/shard_map/all_gather | solution.py:133
  9.0 6.2 %collective-permute-start = (f32[1,64,128]{2,1,0:T(8,128)S(1)}, f32[1,64,128]{2,1,0:T(8,128)S(1)}, u32[]{:S(2)}, u32[]{:S(2)}) collective-permute-start(f32[1,64,128]{2,1,0:T(8,128)S(1)} %slice.828), channel_id=1, source_target_pairs={{0,1},{1,0},{2,3},{3,2},{4,5},{5,4},{6,7},{7,6},{8,9},{9,8},{10,11... | collective-permute-start | bytes 98312 | tf_op jit(solution)/shard_map/ppermute | solution.py:12
  13.6 0.6 copy-start.8
  14.9 49.2 %copy-start.10 = (f32[1,8,64]{2,1,0:T(8,128)}, f32[1,8,64]{2,1,0:T(8,128)S(1)}, u32[]{:S(2)}) copy-start(f32[1,8,64]{2,1,0:T(8,128)S(1)} %get-tuple-element.155) | copy-start | bytes 6148
  14.9 49.2 %copy-start.12 = (f32[1,8,64]{2,1,0:T(8,128)}, f32[1,8,64]{2,1,0:T(8,128)S(1)}, u32[]{:S(2)}) copy-start(f32[1,8,64]{2,1,0:T(8,128)S(1)} %get-tuple-element.156) | copy-start | bytes 6148
  15.2 58.3 %copy-start.7 = (f32[8,256]{1,0:T(8,128)S(1)}, f32[8,256]{1,0:T(8,128)}, u32[]{:S(2)}) copy-start(f32[8,256]{1,0:T(8,128)} %param.9) | copy-start | bytes 24580
  15.2 5.3 %collective-permute-start.1 = (f32[2,64,128]{2,1,0:T(8,128)S(1)}, f32[2,64,128]{2,1,0:T(8,128)S(1)}, u32[]{:S(2)}, u32[]{:S(2)}) collective-permute-start(f32[2,64,128]{2,1,0:T(8,128)S(1)} %maximum_select_fusion.4), channel_id=1, source_target_pairs={{0,2},{1,3},{2,0},{3,1},{4,6},{5,7},{6,4},{7,5},{8,10},{9,11},{10,... | collective-permute-start | bytes 196616 | tf_op jit(solution)/shard_map/ppermute | solution.py:12
  20.6 43.6 %collective-permute-start.2 = (f32[4,64,128]{2,1,0:T(8,128)S(1)}, f32[4,64,128]{2,1,0:T(8,128)S(1)}, u32[]{:S(2)}, u32[]{:S(2)}) collective-permute-start(f32[4,64,128]{2,1,0:T(8,128)S(1)} %maximum_select_fusion.3), channel_id=1, source_target_pairs={{0,4},{1,5},{2,6},{3,7},{4,0},{5,1},{6,2},{7,3},{8,12},{9,13},{10,... | collective-permute-start | bytes 393224 | tf_op jit(solution)/shard_map/ppermute | solution.py:12
  64.2 9.0 %collective-permute-start.3 = (f32[8,64,128]{2,1,0:T(8,128)S(1)}, f32[8,64,128]{2,1,0:T(8,128)S(1)}, u32[]{:S(2)}, u32[]{:S(2)}) collective-permute-start(f32[8,64,128]{2,1,0:T(8,128)S(1)} %maximum_select_fusion.2), channel_id=1, source_target_pairs={{0,8},{1,9},{2,10},{3,11},{4,12},{5,13},{6,14},{7,15},{8,0},{9,1},... | collective-permute-start | bytes 786440 | tf_op jit(solution)/shard_map/ppermute | solution.py:12
  73.2 27.0 %collective-permute-start.4 = (f32[16,64,128]{2,1,0:T(8,128)S(1)}, f32[16,64,128]{2,1,0:T(8,128)S(1)}, u32[]{:S(2)}, u32[]{:S(2)}) collective-permute-start(f32[16,64,128]{2,1,0:T(8,128)S(1)} %maximum_select_fusion.1), channel_id=1, source_target_pairs={{0,16},{1,17},{2,18},{3,19},{4,20},{5,21},{6,22},{7,23},{8,24},{9,... | collective-permute-start | bytes 1572872 | tf_op jit(solution)/shard_map/ppermute | solution.py:12
  103.5 3.2 %copy-start.2 = (f32[32,64,256]{2,1,0:T(8,128)S(1)}, f32[32,64,256]{2,1,0:T(8,128)}, u32[]{:S(2)}) copy-start(f32[32,64,256]{2,1,0:T(8,128)} %all-gather.5.cloned.1.call-done) | copy-start | bytes 6291460
  107.1 29.2 %copy-start.14 = (f32[1,8,64]{2,1,0:T(8,128)S(1)}, f32[1,8,64]{2,1,0:T(8,128)}, u32[]{:S(2)}) copy-start(f32[1,8,64]{2,1,0:T(8,128)} %get-tuple-element.149) | copy-start | bytes 6148
  107.1 29.2 %copy-start.15 = (f32[1,8,64]{2,1,0:T(8,128)S(1)}, f32[1,8,64]{2,1,0:T(8,128)}, u32[]{:S(2)}) copy-start(f32[1,8,64]{2,1,0:T(8,128)} %get-tuple-element.150) | copy-start | bytes 6148
  107.1 29.2 %copy-start.16 = (f32[1,8,64]{2,1,0:T(8,128)S(1)}, f32[1,8,64]{2,1,0:T(8,128)}, u32[]{:S(2)}) copy-start(f32[1,8,64]{2,1,0:T(8,128)} %get-tuple-element.151) | copy-start | bytes 6148
  107.1 29.2 %copy-start.17 = (f32[1,8,64]{2,1,0:T(8,128)S(1)}, f32[1,8,64]{2,1,0:T(8,128)}, u32[]{:S(2)}) copy-start(f32[1,8,64]{2,1,0:T(8,128)} %get-tuple-element.152) | copy-start | bytes 6148
  133.9 8.2 %copy-start.1 = (f32[32,128,128]{2,1,0:T(8,128)S(1)}, f32[32,128,128]{2,1,0:T(8,128)}, u32[]{:S(2)}) copy-start(f32[32,128,128]{2,1,0:T(8,128)} %all-gather.3.cloned.1.call-done) | copy-start | bytes 6291460
  144.7 1.5 copy-start.3
  144.7 1.9 %copy-start.11 = (f32[1,8,64]{2,1,0:T(8,128)S(1)}, f32[1,8,64]{2,1,0:T(8,128)}, u32[]{:S(2)}) copy-start(f32[1,8,64]{2,1,0:T(8,128)} %copy-done.10) | copy-start | bytes 6148
  144.7 1.9 %copy-start.13 = (f32[1,8,64]{2,1,0:T(8,128)S(1)}, f32[1,8,64]{2,1,0:T(8,128)}, u32[]{:S(2)}) copy-start(f32[1,8,64]{2,1,0:T(8,128)} %copy-done.12) | copy-start | bytes 6148
  144.7 2.8 %copy-start.9 = (f32[2,8,64]{2,1,0:T(8,128)S(1)}, f32[2,8,64]{2,1,0:T(8,128)}, u32[]{:S(2)}) copy-start(f32[2,8,64]{2,1,0:T(8,128)} %copy-done.8) | copy-start | bytes 12292
  148.2 0.8 copy-start.6
Sparse Core Ops, SparseCore 0:
  10.2 59.9 all-gather.4
  73.0 60.8 all-gather.2
